TPU v7x, 256 devices: a whole 4x4x8 slice. The times are simulated.
256 devices in a mesh: section: 4 (over x), dp: 8 (over y, core), expert: 8 (over z).
Axes of the slice: x: 4, y: 4, z: 8, core: 2. Of those that a mesh axis runs over, the one named last changes fastest.
Arguments:
- patches: bfloat16 [32768, 1152], P(('dp', 'expert')), may hold values from -50 to 50
- lengths: int32 [64, 4], P(('dp', 'expert')), may hold values from 1 to 64, 128 in all within a row
- w_qkv: bfloat16 [1152, 3456], P(None, 'section'), may hold values from -4.714045 to 4.714045
- w_out: bfloat16 [1152, 1152], P('section'), may hold values from -0.1875 to 0.1875
- w_proj: bfloat16 [4608, 2048], P('dp', 'section'), may hold values from -0.09375 to 0.09375
- routes: int32 [8192, 6], P(('dp', 'expert')), may hold values from 0 to 63, all different within a row; in each aligned block of 128 rows (0 to 127, 128 to 255, ...) at most 24 rows name the same one
- gates: float32 [8192, 6], P(('dp', 'expert')), may hold values from 0.05 to 0.4
- w_gate: bfloat16 [64, 2048, 1408], P(('dp', 'expert'), None, 'section'), may hold values from -0.125 to 0.125
- w_up: bfloat16 [64, 2048, 1408], P(('dp', 'expert'), None, 'section'), may hold values from -0.125 to 0.125
- w_down: bfloat16 [64, 1408, 2048], P(('dp', 'expert'), 'section'), may hold values from -0.15625 to 0.15625
Outputs:
- language_out: bfloat16 [8192, 2048], P(('dp', 'expert'), 'section')
Inputs may be any that keep to these rules, and one draw needn't show every extreme that they name: Each row lists, in order, the lengths in merged tokens of a group's images; they sum to 128 and the largest is exactly 64. `routes`: A token's 6 experts differ. Among the rows of one device no expert is named more than 24 times, a bound that some block reaches in every draw.
All inputs are finite; a program needn't handle non-finite values.
Results may differ from a plain program's by a relative error of at most 0.012.
Values may be sent and summed in bfloat16 or wider, within the bound.
No kernel may reach another device: no remote copies, remote signals or barrier semaphores. Data moves between devices by JAX's collectives and lax.ppermute only.
A program may use at most 64 MiB of HBM per device.

v0:
```python
import math
import jax
import jax.numpy as jnp
from jax import lax
from jax.sharding import PartitionSpec as P

D_VIT = 1152
HEADS = 16
TOP = 6


def layer_norm(values):
    center = values - jnp.mean(values, axis=-1, keepdims=True)
    spread = jnp.mean(center * center, axis=-1, keepdims=True)
    return center * lax.rsqrt(spread + 1e-06)


def rms_norm(values):
    return values * lax.rsqrt(jnp.mean(values * values, axis=-1, keepdims=True) + 1e-06)


def per_device(patches, lengths, w_qkv, w_out, w_proj, routes, gates, w_gate, w_up, w_down):
    data_count = lax.axis_size("dp")
    owner_count = lax.axis_size("expert")
    patch_rows, width = patches.shape
    head_dim = D_VIT // HEADS
    local_heads = w_qkv.shape[1] // (3 * head_dim)
    scale = 1.0 / math.sqrt(head_dim)
    normed_in = layer_norm(patches.astype(jnp.float32)).astype(jnp.bfloat16)
    packed = jnp.dot(normed_in, w_qkv, preferred_element_type=jnp.float32).astype(jnp.bfloat16)
    packed = packed.reshape(patch_rows, local_heads, 3, head_dim)
    query = packed[:, :, 0]
    key_part = packed[:, :, 1]
    value_part = packed[:, :, 2]
    ends = jnp.cumsum(lengths[0]) * 4
    places = jnp.arange(patch_rows, dtype=jnp.int32)
    segment = jnp.sum((places[:, None] >= ends[None, :]).astype(jnp.int32), axis=1)
    block_rows = min(patch_rows, 512)
    block_count = patch_rows // block_rows

    def attend(blocks):
        query_block, segment_block = blocks
        scores = (
            jnp.einsum("qhd,khd->hqk", query_block, key_part, preferred_element_type=jnp.float32)
            * scale
        )
        same = segment_block[:, None] == segment[None, :]
        scores = jnp.where(same[None], scores, -jnp.inf)
        peak = jnp.max(scores, axis=-1, keepdims=True)
        weights = jnp.where(same[None], jnp.exp(scores - peak), 0.0)
        probs = (weights / jnp.sum(weights, axis=-1, keepdims=True)).astype(jnp.bfloat16)
        result = jnp.einsum("hqk,khd->qhd", probs, value_part, preferred_element_type=jnp.float32)
        return result.astype(jnp.bfloat16).reshape(block_rows, local_heads * head_dim)

    attended = lax.map(
        attend,
        (
            query.reshape(block_count, block_rows, local_heads, head_dim),
            segment.reshape(block_count, block_rows),
        ),
    )
    attended = attended.reshape(patch_rows, local_heads * head_dim)
    merged_count = patch_rows // 4
    summed = lax.psum(
        jnp.dot(attended, w_out, preferred_element_type=jnp.float32).astype(jnp.bfloat16), "section"
    ).astype(jnp.float32)
    merged = (
        (patches.astype(jnp.float32) + summed).reshape(merged_count, 4 * width).astype(jnp.bfloat16)
    )
    proj_own = jnp.dot(
        merged, lax.all_gather(w_proj, "dp", axis=0, tiled=True), preferred_element_type=jnp.float32
    ).astype(jnp.bfloat16)
    projected = lax.all_gather(proj_own, "section", axis=1, tiled=True)
    model_width = projected.shape[1]
    normed_tokens = rms_norm(projected.astype(jnp.float32)).astype(jnp.bfloat16)
    expert_total = data_count * owner_count
    capacity = max(2, min(merged_count, 2 * merged_count * TOP // expert_total))
    route_flat = routes.reshape(-1)
    onehot = (route_flat[:, None] == jnp.arange(expert_total, dtype=jnp.int32)[None, :]).astype(
        jnp.int32
    )
    ranks = jnp.cumsum(onehot, axis=0) - 1
    slots = jnp.sum(ranks * onehot, axis=1)
    target = route_flat * capacity + slots
    owners = jnp.arange(merged_count * TOP, dtype=jnp.int32) // TOP
    source = jnp.zeros((expert_total * capacity,), dtype=jnp.int32).at[target].set(owners)
    outgoing = normed_tokens[source].reshape(expert_total, capacity, model_width)
    received = lax.all_to_all(outgoing, ("dp", "expert"), split_axis=0, concat_axis=0, tiled=True)
    flat_rows = received.reshape(-1, received.shape[-1])
    gate_act = jnp.dot(flat_rows, w_gate[0], preferred_element_type=jnp.float32)
    up_act = jnp.dot(flat_rows, w_up[0], preferred_element_type=jnp.float32)
    hidden = (jax.nn.silu(gate_act) * up_act).astype(jnp.bfloat16)
    result = jnp.dot(hidden, w_down[0], preferred_element_type=jnp.float32).astype(jnp.bfloat16)
    returned = lax.all_to_all(
        result.reshape(received.shape[:-1] + (w_down.shape[2],)),
        ("dp", "expert"),
        split_axis=0,
        concat_axis=0,
        tiled=True,
    )
    picked = returned.reshape(expert_total * capacity, model_width)[target].reshape(
        merged_count, TOP, model_width
    )
    weighted = jnp.zeros((merged_count, model_width), dtype=jnp.float32)
    for choice_index in range(TOP):
        weighted = weighted + gates[:, choice_index : choice_index + 1] * picked[
            :, choice_index
        ].astype(jnp.float32)
    expert_cols = lax.psum_scatter(
        weighted.astype(jnp.bfloat16), "section", scatter_dimension=1, tiled=True
    ).astype(jnp.float32)
    return (proj_own.astype(jnp.float32) + expert_cols).astype(jnp.bfloat16)


def solution(mesh):
    return jax.shard_map(
        per_device,
        mesh=mesh,
        in_specs=(
            P(("dp", "expert"), None),
            P(("dp", "expert"), None),
            P(None, "section"),
            P("section", None),
            P("dp", "section"),
            P(("dp", "expert"), None),
            P(("dp", "expert"), None),
            P(("dp", "expert"), None, "section"),
            P(("dp", "expert"), None, "section"),
            P(("dp", "expert"), "section", None),
        ),
        out_specs=P(("dp", "expert"), "section"),
        check_vma=False,
    )
```

profile of v0, /device:TPU:8, one launch (start us, length us, event | category | flops | bytes accessed | tf_op | source)
XLA Modules:
  0.0 488.4 jit_solution(8950288940394244735)
XLA Ops:
  7.4 1.6 convert_reduce_fusion
  9.0 1.7 fusion.5
  11.3 2.4 convolution_convert_fusion.2
  13.7 4.9 %fusion.46 = (f32[4,512]{1,0:T(4,128)S(1)}, f32[4,512,512]{1,2,0:T(8,128)}) fusion(pred[512,512]{0,1:T(8,128)(4,1)S(1)} %broadcast_compare_fusion, bf16[512,4,3,72]{0,3,2,1:T(8,128)(2,1)} %bitcast.124), kind=kOutput, calls=%fused_computation.101 | convolution fusion | flops 156238336 | bytes 5316608 | tf_op jit(solution)/shard_map/while/body/eval_jaxpr/sub | solution.py:50
  18.7 2.8 fusion.16
  21.5 1.9 convolution_convert_fusion.1
  24.5 1.8 reduce-window.19
  27.0 3.4 scatter_custom_fusion
  30.4 47.7 %all-reduce.2.cloned.1.call-done = bf16[512,1152]{1,0:T(8,128)(2,1)} async-done(((bf16[512,1152]{1,0:T(8,128)(2,1)}), bf16[512,1152]{1,0:T(8,128)(2,1)}) %all-reduce.2.cloned.1.call-update) | async-done | bytes 1179664 | tf_op jit(solution)/shard_map/psum | solution.py:64
  80.5 3.1 convolution_convert_fusion.3
  83.6 13.5 %all_gather.7 = bf16[128,2048]{1,0:T(8,128)(2,1)S(1)} all-gather(bf16[128,512]{1,0:T(8,128)(2,1)S(1)} %convolution_convert_fusion.3), channel_id=1, replica_groups=mesh['section'=4,'dp'=8,'expert'=8] {'section'}, dimensions={1}, use_global_device_ids=true | all-gather | bytes 655360 | tf_op jit(solution)/shard_map/all_gather | solution.py:73
  97.4 7.1 %gather_fusion = bf16[1536,2048]{1,0:T(8,128)(2,1)} fusion(bf16[128,2048]{1,0:T(8,128)(2,1)S(1)} %fusion.21, s32[2048]{0:T(1024)S(1)} %pad_clamp_fusion), kind=kCustom, calls=%fused_computation | custom fusion | bytes 12589056 | tf_op jit(solution)/shard_map/gather | solution.py:87
  104.5 150.8 %all_to_all.10 = bf16[64,24,2048]{2,1,0:T(8,128)(2,1)S(1)} all-to-all(bf16[64,24,2048]{2,1,0:T(8,128)(2,1)} %bitcast.118), channel_id=1, replica_groups=mesh['section'=4,'dp'=8,'expert'=8] {'dp','expert'}, dimensions={0} | all-to-all | bytes 12582912 | tf_op jit(solution)/shard_map/all_to_all | solution.py:88
  255.3 2.7 copy-done.3
  258.0 3.8 fusion.14
  261.8 11.8 %convolution_convert_fusion = bf16[1536,2048]{1,0:T(8,128)(2,1)} fusion(bf16[1,352,2048]{2,1,0:T(8,128)(2,1)S(1)} %copy-done.7, bf16[1536,2048]{1,0:T(8,128)(2,1)} %bitcast.121, f32[1536,352]{0,1:T(8,128)} %fusion.14, bf16[1,2048,352]{1,2,0:T(8,128)(2,1)} %param.18), kind=kOutput, calls=%fused_computation.4 | convolution fusion | flops 4435574784 | bytes 17629184 | tf_op jit(solution)/shard_map/dot_general | solution.py:93
  273.6 7.5 %all-to-all-start.1 = ((bf16[64,24,2048]{2,1,0:T(8,128)(2,1)}), bf16[64,24,2048]{2,1,0:T(8,128)(2,1)}, u32[]{:S(2)}, u32[]{:S(2)}) async-start(bf16[64,24,2048]{2,1,0:T(8,128)(2,1)} %bitcast.119), calls=%async_computation.1 | async-start | bytes 12582912 | tf_op jit(solution)/shard_map/all_to_all | solution.py:94
  281.4 138.7 %all-to-all-done.1 = bf16[64,24,2048]{2,1,0:T(8,128)(2,1)} async-done(((bf16[64,24,2048]{2,1,0:T(8,128)(2,1)}), bf16[64,24,2048]{2,1,0:T(8,128)(2,1)}, u32[]{:S(2)}, u32[]{:S(2)}) %all-to-all-start.1) | async-done | bytes 6291488 | tf_op jit(solution)/shard_map/all_to_all | solution.py:94
  420.1 10.7 %gather_fusion.1 = bf16[768,2048]{1,0:T(8,128)(2,1)} fusion(bf16[1536,2048]{1,0:T(8,128)(2,1)} %bitcast.16, s32[1024]{0:T(1024)S(1)} %pad_clamp_fusion.1), kind=kCustom, calls=%fused_computation.1 | custom fusion | bytes 6294528 | tf_op jit(solution)/shard_map/gather | solution.py:101
  430.8 6.3 %reshape.176 = bf16[128,6,2048]{2,1,0:T(8,128)(2,1)} reshape(bf16[768,2048]{1,0:T(8,128)(2,1)} %gather_fusion.1) | data formatting | bytes 6291456 | tf_op jit(solution)/shard_map/reshape | solution.py:101
  437.1 15.9 %fusion.45 = (bf16[128,1,2048]{2,1,0:T(2,128)(2,1)S(1)}, bf16[128,1,2048]{2,1,0:T(2,128)(2,1)S(1)}, bf16[128,1,2048]{2,1,0:T(2,128)(2,1)S(1)}, bf16[128,1,2048]{...) fusion(bf16[128,6,2048]{2,1,0:T(8,128)(2,1)} %reshape.176), kind=kLoop, calls=%fused_computation.100 | loop fusion | bytes 6291456 | tf_op jit(solution)/shard_map/slice | solution.py:106
  453.1 4.2 fusion.23
  457.3 22.1 %reduce-scatter.2.cloned.1.call-done = bf16[128,512]{1,0:T(8,128)(2,1)} async-done(((bf16[128,2048]{1,0:T(8,128)(2,1)}), bf16[128,512]{1,0:T(8,128)(2,1)}) %reduce-scatter.2.cloned.1.call-update) | async-done | bytes 131088 | tf_op jit(solution)/shard_map/reduce_scatter | solution.py:109
  479.4 1.6 add_convert_fusion
  (53 shorter events, 5.3 us)
Async XLA Ops:
  7.4 3.9 copy-start
  7.4 3.9 copy-start.2
  7.4 3.4 copy-start.9
  7.4 70.7 %all-reduce.2.cloned.1.call-start = ((), (), s32[]{:S(2)}) async-start(), calls=%async_computation.3 | async-start | bytes 2359296 | tf_op jit(solution)/shard_map/psum | solution.py:64
  18.7 2.9 copy-start.8
  21.5 2.5 copy-start.4
  23.5 57.0 %all-gather.2.cloned.1.call-start = ((), (), s32[]{:S(2)}) async-start(), calls=%async_computation.4 | async-start | bytes 5308416 | tf_op jit(solution)/shard_map/all_gather | solution.py:71
  104.5 153.4 %copy-start.6 = (bf16[1,2048,352]{1,2,0:T(8,128)(2,1)S(1)}, bf16[1,2048,352]{1,2,0:T(8,128)(2,1)}, u32[]{:S(2)}) copy-start(bf16[1,2048,352]{1,2,0:T(8,128)(2,1)} %param.17) | copy-start | bytes 4325380
  255.3 2.7 copy-start.3
  258.0 3.8 copy-start.7
  273.6 7.8 %copy-start.5 = (f32[128,6]{0,1:T(8,128)S(1)}, f32[128,6]{0,1:T(8,128)}, u32[]{:S(2)}) copy-start(f32[128,6]{0,1:T(8,128)} %param.16) | copy-start | bytes 9220
  273.6 146.5 %all-to-all-start.1 = ((bf16[64,24,2048]{2,1,0:T(8,128)(2,1)}), bf16[64,24,2048]{2,1,0:T(8,128)(2,1)}, u32[]{:S(2)}, u32[]{:S(2)}) async-start(bf16[64,24,2048]{2,1,0:T(8,128)(2,1)} %bitcast.119), calls=%async_computation.1 | async-start | bytes 12582912 | tf_op jit(solution)/shard_map/all_to_all | solution.py:94
  281.1 198.3 %reduce-scatter.2.cloned.1.call-start = ((), (), s32[]{:S(2)}) async-start(), calls=%async_computation.5 | async-start | bytes 655360 | tf_op jit(solution)/shard_map/reduce_scatter | solution.py:109
  453.0 27.9 %copy-start.1 = (bf16[1152,864]{0,1:T(8,128)(2,1)S(1)}, bf16[1152,864]{0,1:T(8,128)(2,1)}, u32[]{:S(2)}) copy-start(bf16[1152,864]{0,1:T(8,128)(2,1)} %param.12) | copy-start | bytes 5971972
Sparse Core Ops, SparseCore 0:
  23.6 54.4 all-reduce.1
  457.4 21.9 reduce-scatter.1
Sparse Core Ops, SparseCore 1:
  25.8 38.5 all-gather.1
where the time goes:
time: 489 us; the launch traced here: 488 us
  waiting for transfers between devices  209 us (43%)
  blocking collectives  164 us (34%)
  local copies, waits for them, and re-layouts  47.7 us (10%)
  matrix products  30.9 us (6%)
  between operations  15.1 us (3%)
  other arithmetic  13.7 us (3%)
  starting transfers between devices  7.77 us (2%)
    all_to_all x1, blocking collectives, per_device(): lax.all_to_all(outgoing, ('dp', 'expert'), split_axis=0, concat_axis=0, t...  151 us
    all_to_all x1, waiting for transfers between devices, per_device(): lax.all_to_all(result.reshape(received.shape[:-1] + (w_down.shape[2],)),...  139 us
    psum x1, waiting for transfers between devices, per_device(): lax.psum(jnp.dot(attended, w_out, preferred_element_type=jnp.float32).ast...  47.7 us
    reduce_scatter x1, waiting for transfers between devices, per_device(): lax.psum_scatter(weighted.astype(jnp.bfloat16), 'section', scatter_dimens...  22.1 us
    slice x1, local copies, waits for them, and re-layouts, per_device(): picked[:, choice_index].astype(jnp.float32)  15.9 us
    all_gather x1, blocking collectives, per_device(): projected = lax.all_gather(proj_own, 'section', axis=1, tiled=True)  13.5 us
    dot_general x1, matrix products, per_device(): jnp.dot(hidden, w_down[0], preferred_element_type=jnp.float32)  11.8 us
    gather x1, local copies, waits for them, and re-layouts, per_device(): returned.reshape(expert_total * capacity, model_width)[target]  10.7 us
  transfers between devices with their start and end apart: 4, of which 3 were waited for; matrix products, arithmetic and copies ran while one was open for 2% of the time, Pallas kernels for 0%

commit v1 on v0

--- a/solution.py
+++ b/solution.py
@@ -7,6 +7,11 @@
 D_VIT = 1152
 HEADS = 16
 TOP = 6
+
+
+def add_all(x, axis):
+    terms = lax.all_gather(x, axis)
+    return jnp.sum(terms, axis=0)
 
 
 def layer_norm(values):
@@ -61,7 +66,7 @@
     )
     attended = attended.reshape(patch_rows, local_heads * head_dim)
     merged_count = patch_rows // 4
-    summed = lax.psum(
+    summed = add_all(
         jnp.dot(attended, w_out, preferred_element_type=jnp.float32).astype(jnp.bfloat16), "section"
     ).astype(jnp.float32)
     merged = (

time: 489 us -> 527 us (1.078)
  waiting for transfers between devices: 209 us -> 245 us
    all_gather x0 -> x1, waiting for transfers between devices: none -> 51 us  [add_all(): terms = lax.all_gather(x, axis)]
    psum x1 -> x0, waiting for transfers between devices: 47.7 us -> none  [per_device(): lax.psum(jnp.dot(attended, w_out, preferred_element_type=jnp.float32).ast...]
    all_gather x1, waiting for transfers between devices: 0.03 us -> 31.4 us  [per_device(): lax.all_gather(w_proj, 'dp', axis=0, tiled=True)]
  transfers between devices with their start and end apart: 4 -> 4, of which waited for: 3 -> 4; matrix products, arithmetic and copies ran while one was open for 2% -> 2% of each run, Pallas kernels for 0% -> 0%
where the time goes in v1:
time: 527 us; the launch traced here: 526 us
  waiting for transfers between devices  245 us (46%)
  blocking collectives  164 us (31%)
  local copies, waits for them, and re-layouts  47.7 us (9%)
  matrix products  30.8 us (6%)
  other arithmetic  18 us (3%)
  between operations  13.3 us (3%)
  starting transfers between devices  7.55 us (1%)
    all_to_all x1, blocking collectives, per_device(): lax.all_to_all(outgoing, ('dp', 'expert'), split_axis=0, concat_axis=0, t...  151 us
    all_to_all x1, waiting for transfers between devices, per_device(): lax.all_to_all(result.reshape(received.shape[:-1] + (w_down.shape[2],)),...  139 us
    all_gather x1, waiting for transfers between devices, add_all(): terms = lax.all_gather(x, axis)  51 us
    all_gather x1, waiting for transfers between devices, per_device(): lax.all_gather(w_proj, 'dp', axis=0, tiled=True)  31.4 us
    reduce_scatter x1, waiting for transfers between devices, per_device(): lax.psum_scatter(weighted.astype(jnp.bfloat16), 'section', scatter_dimens...  23.3 us
    slice x1, local copies, waits for them, and re-layouts, per_device(): picked[:, choice_index].astype(jnp.float32)  15.9 us
    all_gather x1, blocking collectives, per_device(): projected = lax.all_gather(proj_own, 'section', axis=1, tiled=True)  13.1 us
    dot_general x1, matrix products, per_device(): jnp.dot(hidden, w_down[0], preferred_element_type=jnp.float32)  11.8 us
  transfers between devices with their start and end apart: 4, of which 4 were waited for; matrix products, arithmetic and copies ran while one was open for 2% of the time, Pallas kernels for 0%

profile of v1, /device:TPU:8, one launch (start us, length us, event | category | flops | bytes accessed | tf_op | source)
XLA Modules:
  0.0 526.4 jit_solution(14866957658823767984)
XLA Ops:
  8.2 1.7 fusion.5
  10.5 2.4 convolution_convert_fusion.2
  12.9 4.9 fusion.46
  17.9 2.8 fusion.16
  20.7 1.9 convolution_convert_fusion.1
  23.8 1.8 reduce-window.19
  26.3 3.4 scatter_custom_fusion
  29.7 51.0 %all-gather.6.cloned.1.call-done = bf16[2048,1152]{1,0:T(8,128)(2,1)} async-done(((bf16[512,1152]{1,0:T(8,128)(2,1)}), bf16[2048,1152]{1,0:T(8,128)(2,1)}) %all-gather.6.cloned.1.call-update) | async-done | bytes 4718608 | tf_op jit(solution)/shard_map/all_gather | solution.py:13
  80.7 4.4 reduce_sum.73
  87.4 31.4 %all-gather.4.cloned.1.call-done = bf16[4608,512]{1,0:T(8,128)(2,1)} async-done(((bf16[576,512]{1,0:T(8,128)(2,1)}), bf16[4608,512]{1,0:T(8,128)(2,1)}) %all-gather.4.cloned.1.call-update) | async-done | bytes 4718608 | tf_op jit(solution)/shard_map/all_gather | solution.py:76
  118.9 3.1 convolution_convert_fusion.3
  122.0 13.1 %all_gather.15 = bf16[128,2048]{1,0:T(8,128)(2,1)S(1)} all-gather(bf16[128,512]{1,0:T(8,128)(2,1)S(1)} %convolution_convert_fusion.3), channel_id=1, replica_groups=mesh['section'=4,'dp'=8,'expert'=8] {'section'}, dimensions={1}, use_global_device_ids=true | all-gather | bytes 655360 | tf_op jit(solution)/shard_map/all_gather | solution.py:78
  135.4 7.1 %gather_fusion = bf16[1536,2048]{1,0:T(8,128)(2,1)} fusion(bf16[128,2048]{1,0:T(8,128)(2,1)S(1)} %fusion.21, s32[2048]{0:T(1024)S(1)} %pad_clamp_fusion), kind=kCustom, calls=%fused_computation | custom fusion | bytes 12589056 | tf_op jit(solution)/shard_map/gather | solution.py:92
  142.5 150.5 %all_to_all.10 = bf16[64,24,2048]{2,1,0:T(8,128)(2,1)S(1)} all-to-all(bf16[64,24,2048]{2,1,0:T(8,128)(2,1)} %bitcast.119), channel_id=1, replica_groups=mesh['section'=4,'dp'=8,'expert'=8] {'dp','expert'}, dimensions={0} | all-to-all | bytes 12582912 | tf_op jit(solution)/shard_map/all_to_all | solution.py:93
  293.0 2.7 copy-done.3
  295.7 3.8 fusion.14
  299.5 11.8 %convolution_convert_fusion = bf16[1536,2048]{1,0:T(8,128)(2,1)} fusion(bf16[1,352,2048]{2,1,0:T(8,128)(2,1)S(1)} %copy-done.7, bf16[1536,2048]{1,0:T(8,128)(2,1)} %bitcast.122, f32[1536,352]{0,1:T(8,128)} %fusion.14, bf16[1,2048,352]{1,2,0:T(8,128)(2,1)} %param.18), kind=kOutput, calls=%fused_computation.4 | convolution fusion | flops 4435574784 | bytes 17629184 | tf_op jit(solution)/shard_map/dot_general | solution.py:98
  311.3 7.5 %all-to-all-start.1 = ((bf16[64,24,2048]{2,1,0:T(8,128)(2,1)}), bf16[64,24,2048]{2,1,0:T(8,128)(2,1)}, u32[]{:S(2)}, u32[]{:S(2)}) async-start(bf16[64,24,2048]{2,1,0:T(8,128)(2,1)} %bitcast.120), calls=%async_computation.1 | async-start | bytes 12582912 | tf_op jit(solution)/shard_map/all_to_all | solution.py:99
  318.9 138.9 %all-to-all-done.1 = bf16[64,24,2048]{2,1,0:T(8,128)(2,1)} async-done(((bf16[64,24,2048]{2,1,0:T(8,128)(2,1)}), bf16[64,24,2048]{2,1,0:T(8,128)(2,1)}, u32[]{:S(2)}, u32[]{:S(2)}) %all-to-all-start.1) | async-done | bytes 6291488 | tf_op jit(solution)/shard_map/all_to_all | solution.py:99
  457.8 10.7 %gather_fusion.1 = bf16[768,2048]{1,0:T(8,128)(2,1)} fusion(bf16[1536,2048]{1,0:T(8,128)(2,1)} %bitcast.17, s32[1024]{0:T(1024)S(1)} %pad_clamp_fusion.1), kind=kCustom, calls=%fused_computation.1 | custom fusion | bytes 6294528 | tf_op jit(solution)/shard_map/gather | solution.py:106
  468.5 6.3 %reshape.176 = bf16[128,6,2048]{2,1,0:T(8,128)(2,1)} reshape(bf16[768,2048]{1,0:T(8,128)(2,1)} %gather_fusion.1) | data formatting | bytes 6291456 | tf_op jit(solution)/shard_map/reshape | solution.py:106
  474.8 15.9 %fusion.45 = (bf16[128,1,2048]{2,1,0:T(2,128)(2,1)S(1)}, bf16[128,1,2048]{2,1,0:T(2,128)(2,1)S(1)}, bf16[128,1,2048]{2,1,0:T(2,128)(2,1)S(1)}, bf16[128,1,2048]{...) fusion(bf16[128,6,2048]{2,1,0:T(8,128)(2,1)} %reshape.176), kind=kLoop, calls=%fused_computation.100 | loop fusion | bytes 6291456 | tf_op jit(solution)/shard_map/slice | solution.py:111
  490.8 4.2 fusion.23
  495.0 23.3 %reduce-scatter.2.cloned.1.call-done = bf16[128,512]{1,0:T(8,128)(2,1)} async-done(((bf16[128,2048]{1,0:T(8,128)(2,1)}), bf16[128,512]{1,0:T(8,128)(2,1)}) %reduce-scatter.2.cloned.1.call-update) | async-done | bytes 131088 | tf_op jit(solution)/shard_map/reduce_scatter | solution.py:114
  (54 shorter events, 8.4 us)
Async XLA Ops:
  6.5 3.9 copy-start
  6.5 3.9 copy-start.2
  6.5 3.4 copy-start.9
  6.5 74.2 %all-gather.6.cloned.1.call-start = ((), (), s32[]{:S(2)}) async-start(), calls=%async_computation.5 | async-start | bytes 5898240 | tf_op jit(solution)/shard_map/all_gather | solution.py:13
  17.9 2.9 copy-start.8
  20.7 2.7 copy-start.4
  22.6 96.3 %all-gather.4.cloned.1.call-start = ((), (), s32[]{:S(2)}) async-start(), calls=%async_computation.3 | async-start | bytes 5308416 | tf_op jit(solution)/shard_map/all_gather | solution.py:76
  142.5 153.2 %copy-start.6 = (bf16[1,2048,352]{1,2,0:T(8,128)(2,1)S(1)}, bf16[1,2048,352]{1,2,0:T(8,128)(2,1)}, u32[]{:S(2)}) copy-start(bf16[1,2048,352]{1,2,0:T(8,128)(2,1)} %param.17) | copy-start | bytes 4325380
  293.0 2.7 copy-start.3
  295.7 3.8 copy-start.7
  311.3 7.5 %copy-start.5 = (f32[128,6]{0,1:T(8,128)S(1)}, f32[128,6]{0,1:T(8,128)}, u32[]{:S(2)}) copy-start(f32[128,6]{0,1:T(8,128)} %param.16) | copy-start | bytes 9220
  311.3 146.5 %all-to-all-start.1 = ((bf16[64,24,2048]{2,1,0:T(8,128)(2,1)}), bf16[64,24,2048]{2,1,0:T(8,128)(2,1)}, u32[]{:S(2)}, u32[]{:S(2)}) async-start(bf16[64,24,2048]{2,1,0:T(8,128)(2,1)} %bitcast.120), calls=%async_computation.1 | async-start | bytes 12582912 | tf_op jit(solution)/shard_map/all_to_all | solution.py:99
  318.8 199.5 %reduce-scatter.2.cloned.1.call-start = ((), (), s32[]{:S(2)}) async-start(), calls=%async_computation.4 | async-start | bytes 655360 | tf_op jit(solution)/shard_map/reduce_scatter | solution.py:114
  490.7 29.2 %copy-start.1 = (bf16[1152,864]{0,1:T(8,128)(2,1)S(1)}, bf16[1152,864]{0,1:T(8,128)(2,1)}, u32[]{:S(2)}) copy-start(bf16[1152,864]{0,1:T(8,128)(2,1)} %param.12) | copy-start | bytes 5971972
Sparse Core Ops, SparseCore 0:
  22.7 57.9 all-gather.5
  82.6 36.2 all-gather.3
  495.1 23.1 reduce-scatter.1
